TPU v7x, 32 devices: a whole 2x2x4 slice. The times are simulated.
32 devices in a mesh: seq: 8 (over z, x), head: 4 (over y, core).
Axes of the slice: x: 2, y: 2, z: 4, core: 2. Of those that a mesh axis runs over, the one named last changes fastest.
Arguments:
- h_in: float32 [2048, 1024], P('seq', 'head'), may hold values from -6 to 6
- norm_gain: float32 [2, 1024], P(None, 'head'), may hold values from 0.5 to 1.5
- w_z: bfloat16 [2, 1024, 2048], P(None, None, 'head'), may hold values from -0.1875 to 0.1875
- w_x: bfloat16 [2, 1024, 2048], P(None, None, 'head'), may hold values from -0.1875 to 0.1875
- w_bc: bfloat16 [2, 1024, 256], replicated, may hold values from -0.1875 to 0.1875
- w_dt: bfloat16 [2, 1024, 32], P(None, None, 'head'), may hold values from -0.1875 to 0.1875
- conv_x_w: float32 [2, 4, 2048], P(None, None, 'head'), may hold values from -3 to 3
- conv_x_b: float32 [2, 2048], P(None, 'head'), may hold values from -0.5 to 0.5
- conv_bc_w: float32 [2, 4, 256], replicated, may hold values from -3 to 3
- conv_bc_b: float32 [2, 256], replicated, may hold values from -0.5 to 0.5
- dt_bias: float32 [2, 32], P(None, 'head'), may hold values from -4 to -1
- a_log: float32 [2, 32], P(None, 'head'), may hold values from -10 to -1
- skip: float32 [2, 32], P(None, 'head'), may hold values from 0.5 to 1.5
- gate_gain: float32 [2, 2048], P(None, 'head'), may hold values from 0.5 to 1.5
- w_out: bfloat16 [2, 2048, 1024], P(None, 'head'), may hold values from -0.125 to 0.125
- d_out: float32 [2048, 1024], P('seq', 'head'), may hold values from -6 to 6
Outputs:
- h_out: float32 [2048, 1024], P('seq', 'head')
- d_h: float32 [2048, 1024], P('seq', 'head')
- d_norm_gain: float32 [2, 1024], P(None, 'head')
- d_w_z: float32 [2, 1024, 2048], P(None, 'seq', 'head')
- d_w_x: float32 [2, 1024, 2048], P(None, 'seq', 'head')
- d_w_bc: float32 [2, 1024, 256], replicated
- d_w_dt: float32 [2, 1024, 32], P(None, 'seq', 'head')
- d_conv_x_w: float32 [2, 4, 2048], P(None, None, 'head')
- d_conv_x_b: float32 [2, 2048], P(None, 'head')
- d_conv_bc_w: float32 [2, 4, 256], replicated
- d_conv_bc_b: float32 [2, 256], replicated
- d_dt_bias: float32 [2, 32], P(None, 'head')
- d_a_log: float32 [2, 32], P(None, 'head')
- d_skip: float32 [2, 32], P(None, 'head')
- d_gate_gain: float32 [2, 2048], P(None, 'head')
- d_w_out: float32 [2, 2048, 1024], P(None, 'head', 'seq')
All inputs are finite; a program needn't handle non-finite values.
Results may differ from a plain program's by a relative error of at most 0.014.
The roundings to bfloat16 on the way count: a program that leaves them out, or rounds other values in their place, can miss the bound.
Values may be sent and summed in bfloat16 or wider, within the bound.
A program may use at most 128 MiB of HBM per device.

v0:
```python
import jax
import jax.numpy as jnp
from jax import lax
from jax.sharding import PartitionSpec as P

D = 1024
HEAD_DIM = 64
STATE = 128
CONV = 4
SPAN = 256
LAYERS = 2
DI = 2048
epsilon = 1e-05
highest = lax.Precision.HIGHEST


def shifted(value, axis, steps):
    count = lax.axis_size(axis)
    first, last = (max(0, -steps), min(count, count - steps))
    return lax.ppermute(value, axis, [(source, source + steps) for source in range(first, last)])


def entering_2(value, axis, join, neutral, backward):
    count, mine = (lax.axis_size(axis), lax.axis_index(axis))
    pieces = jax.tree.map(lambda part: lax.all_gather(part, axis), value)
    if backward:
        pieces = jax.tree.map(lambda part: part[::-1], pieces)
        mine = count - 1 - mine
    total = jax.tree.map(
        lambda part, zero: jnp.full_like(part, 0) + jnp.asarray(zero, part.dtype), value, neutral
    )

    def lap(position, total):
        longer = join(total, jax.tree.map(lambda part: part[position], pieces))
        return jax.tree.map(lambda new, old: jnp.where(position < mine, new, old), longer, total)

    return lax.fori_loop(0, count - 1, lap, total)


def conv_inputs(extended, dt_raw, conv_weight, conv_bias, dt_bias, a_log):
    row_count = dt_raw.shape[0]
    mixed = jnp.zeros((row_count, extended.shape[1]), jnp.float32) + conv_bias[None, :]
    for offset in range(CONV):
        mixed = mixed + conv_weight[offset][None, :] * extended[offset : offset + row_count]
    active = jax.nn.silu(mixed)
    inner = extended.shape[1] - 2 * STATE
    head_count = dt_raw.shape[1]
    values = active[:, :inner].reshape(row_count, head_count, HEAD_DIM)
    b_proj = active[:, inner : inner + STATE]
    c_proj = active[:, inner + STATE :]
    steps_dt = jax.nn.softplus(dt_raw + dt_bias[None, :])
    log_decay = -steps_dt * jnp.exp(a_log)[None, :]
    return (values, b_proj, c_proj, steps_dt, log_decay)


def scan_from_zero(values, b_proj, c_proj, steps_dt, log_decay):
    row_count, head_count = steps_dt.shape
    blocks = row_count // SPAN
    causal = (jnp.arange(SPAN)[:, None] >= jnp.arange(SPAN)[None, :])[None]

    def one_block(carried, block_data):
        block_vals, b_blk, c_blk, dt_blk, la_blk = block_data
        cumulative = jnp.cumsum(la_blk, axis=0)
        cum_heads = cumulative.T
        spread = cum_heads[:, :, None] - cum_heads[:, None, :]
        weights = jnp.where(causal, jnp.exp(jnp.where(causal, spread, 0.0)), 0.0)
        scores = jnp.dot(c_blk, b_blk.T, precision=highest)
        scaled = block_vals * dt_blk[:, :, None]
        y_diag = jnp.einsum("htu,uhp->thp", weights * scores[None], scaled, precision=highest)
        y_off = (
            jnp.einsum("tn,hpn->thp", c_blk, carried, precision=highest)
            * jnp.exp(cumulative)[:, :, None]
        )
        ending = cumulative[-1]
        tail_decay = jnp.exp(ending[None, :] - cumulative)
        updated = carried * jnp.exp(ending)[:, None, None] + jnp.einsum(
            "uhp,un->hpn", scaled * tail_decay[:, :, None], b_blk, precision=highest
        )
        return (updated, y_diag + y_off)

    stacked = (
        values.reshape(blocks, SPAN, head_count, HEAD_DIM),
        b_proj.reshape(blocks, SPAN, STATE),
        c_proj.reshape(blocks, SPAN, STATE),
        steps_dt.reshape(blocks, SPAN, head_count),
        log_decay.reshape(blocks, SPAN, head_count),
    )
    initial = jnp.zeros((head_count, HEAD_DIM, STATE), jnp.float32)
    last_state, outputs = lax.scan(one_block, initial, stacked)
    return (outputs.reshape(row_count, head_count, HEAD_DIM), last_state)


def carry_term(c_proj, log_decay, entering):
    cumulative = jnp.cumsum(log_decay, axis=0)
    return (
        jnp.einsum("tn,hpn->thp", c_proj, entering, precision=highest)
        * jnp.exp(cumulative)[:, :, None]
    )


def link_states(earlier, later):
    return (earlier[0] * later[0], later[0][:, None, None] * earlier[1] + later[1])


def token_sums(partial_sums):
    return lax.psum(partial_sums, "head")


def contract_first(left, right):
    return lax.dot_general(
        left, right, (((0,), (0,)), ((), ())), preferred_element_type=jnp.float32
    )


def local(
    h_in,
    norm_gain,
    w_z,
    w_x,
    w_bc,
    w_dt,
    conv_x_w,
    conv_x_b,
    conv_bc_w,
    conv_bc_b,
    dt_bias,
    a_log,
    skip,
    gate_gain,
    w_out,
    d_out,
):
    row_count = h_in.shape[0]
    inner = w_x.shape[2]
    head_count = w_dt.shape[2]
    hidden = h_in
    kept = []
    for layer_idx in range(LAYERS):
        gain_one = norm_gain[layer_idx]
        full_hidden, full_gain = (
            lax.all_gather(hidden, "head", axis=1, tiled=True),
            lax.all_gather(gain_one, "head", axis=0, tiled=True),
        )
        factor = lax.rsqrt(jnp.mean(full_hidden * full_hidden, axis=1) + epsilon)
        normed = (full_hidden * factor[:, None] * full_gain[None, :]).astype(jnp.bfloat16)
        gate_in = jnp.dot(normed, w_z[layer_idx], preferred_element_type=jnp.float32)
        x_in = jnp.dot(normed, w_x[layer_idx], preferred_element_type=jnp.float32)
        bc_in = jnp.dot(normed, w_bc[layer_idx], preferred_element_type=jnp.float32)
        dt_raw = jnp.dot(normed, w_dt[layer_idx], preferred_element_type=jnp.float32)
        conv_in = jnp.concatenate([x_in, bc_in], axis=1)
        before = shifted(conv_in[row_count - (CONV - 1) :], "seq", 1)
        extended = jnp.concatenate([before, conv_in], axis=0)
        conv_weight = jnp.concatenate([conv_x_w[layer_idx], conv_bc_w[layer_idx]], axis=1)
        conv_bias = jnp.concatenate([conv_x_b[layer_idx], conv_bc_b[layer_idx]], axis=0)
        inputs, input_back = jax.vjp(
            conv_inputs,
            extended,
            dt_raw,
            conv_weight,
            conv_bias,
            dt_bias[layer_idx],
            a_log[layer_idx],
        )
        values, b_proj, c_proj, steps_dt, log_decay = inputs
        local_part, block_back = jax.vjp(
            scan_from_zero, values, b_proj, c_proj, steps_dt, log_decay
        )
        scanned, leaving = local_part
        decays = jnp.exp(jnp.sum(log_decay, axis=0))
        identity = (jnp.ones_like(decays), jnp.zeros_like(leaving))
        entering = entering_2((decays, leaving), "seq", link_states, identity, False)[1]
        carried_part, carry_back = jax.vjp(carry_term, c_proj, log_decay, entering)
        mixed = scanned + carried_part + skip[layer_idx][None, :, None] * values
        gate_act = jax.nn.silu(gate_in)
        gated = mixed.reshape(row_count, inner) * gate_act
        gate_factor = lax.rsqrt(token_sums(jnp.sum(gated * gated, axis=1)) / DI + epsilon)
        scaled = (gated * gate_factor[:, None] * gate_gain[layer_idx][None, :]).astype(jnp.bfloat16)
        out_weight = w_out[layer_idx]
        summed = lax.psum_scatter(
            contract_first(out_weight, scaled.T), "head", scatter_dimension=0, tiled=True
        )
        kept.append(
            (
                hidden,
                factor,
                normed,
                gate_in,
                gate_act,
                gated,
                gate_factor,
                scaled,
                mixed,
                values,
                decays,
                entering,
                input_back,
                block_back,
                carry_back,
            )
        )
        hidden = hidden + summed.T
    grad = d_out
    collected = [None] * LAYERS
    for layer_idx in reversed(range(LAYERS)):
        (
            layer_input,
            factor,
            normed,
            gate_in,
            gate_act,
            gated,
            gate_factor,
            scaled,
            mixed,
            values,
            decays,
            entering,
            input_back,
            block_back,
            carry_back,
        ) = kept[layer_idx]
        grad_b = grad.astype(jnp.bfloat16)
        out_weight = w_out[layer_idx]
        grad_cols = lax.all_gather(grad_b, "head", axis=1, tiled=True)
        d_part = lax.dot_general(
            grad_cols, out_weight, (((1,), (1,)), ((), ())), preferred_element_type=jnp.float32
        )
        d_cols = contract_first(scaled, grad_cols)
        normalized = gated * gate_factor[:, None]
        d_ggain = jnp.sum(d_part * normalized, axis=0)
        d_norm_in = d_part * gate_gain[layer_idx][None, :]
        along = token_sums(jnp.sum(d_norm_in * normalized, axis=1)) / DI
        d_gated = gate_factor[:, None] * (d_norm_in - normalized * along[:, None])
        sigma = jax.nn.sigmoid(gate_in)
        d_gate = d_gated * mixed.reshape(row_count, inner) * sigma * (1.0 + gate_in * (1.0 - sigma))
        d_mixed = (d_gated * gate_act).reshape(row_count, head_count, HEAD_DIM)
        d_skipped = jnp.sum(d_mixed * values, axis=(0, 2))
        d_c_carry, d_la_carry, d_entering = carry_back(d_mixed)
        back_identity = (jnp.ones_like(decays), jnp.zeros_like(d_entering))
        leaving_grad = entering_2((decays, d_entering), "seq", link_states, back_identity, True)[1]
        d_decays = jnp.sum(leaving_grad * entering, axis=(1, 2)) * decays
        d_values, d_b_proj, d_c_local, d_steps, d_la_local = block_back((d_mixed, leaving_grad))
        d_values = d_values + skip[layer_idx][None, :, None] * d_mixed
        d_inputs = (
            d_values,
            d_b_proj,
            d_c_carry + d_c_local,
            d_steps,
            d_la_carry + d_la_local + d_decays[None, :],
        )
        d_extended, d_dtraw, d_cweight, d_cbias, d_dtbias, d_alog = input_back(d_inputs)
        returned = shifted(d_extended[: CONV - 1], "seq", -1)
        d_conv = d_extended[CONV - 1 :] + jnp.pad(returned, ((row_count - (CONV - 1), 0), (0, 0)))
        d_gate_b = d_gate.astype(jnp.bfloat16)
        d_x_b = d_conv[:, :inner].astype(jnp.bfloat16)
        d_shared = d_conv[:, inner:]
        d_dt_b = d_dtraw.astype(jnp.bfloat16)
        d_wz = contract_first(normed, d_gate_b)
        d_wx = contract_first(normed, d_x_b)
        d_wdt = contract_first(normed, d_dt_b)
        d_wbc = lax.dot_general(
            normed.astype(jnp.float32), d_shared, (((0,), (0,)), ((), ())), precision=highest
        )
        wz_now = w_z[layer_idx]
        wx_now = w_x[layer_idx]
        wdt_now = w_dt[layer_idx]
        wbc_now = w_bc[layer_idx]

        def product(weight, grads):
            return lax.dot_general(
                weight, grads, (((1,), (1,)), ((), ())), preferred_element_type=jnp.float32
            )

        shared_rows = wbc_now.astype(jnp.float32)
        shared_term = lax.dot_general(
            shared_rows, d_shared, (((1,), (1,)), ((), ())), precision=highest
        )
        d_normed = lax.psum_scatter(
            product(wz_now, d_gate_b)
            + product(wx_now, d_x_b)
            + product(wdt_now, d_dt_b)
            + shared_term,
            "head",
            scatter_dimension=0,
            tiled=True,
        ).T
        centered = layer_input * factor[:, None]
        d_ngain = jnp.sum(d_normed * centered, axis=0)
        d_unit = d_normed * norm_gain[layer_idx][None, :]
        along_in = token_sums(jnp.sum(d_unit * centered, axis=1)) / D
        grad = grad + factor[:, None] * (d_unit - centered * along_in[:, None])
        collected[layer_idx] = (
            d_wz,
            d_wx,
            d_wdt,
            d_cols,
            d_ngain,
            d_cweight[:, :inner],
            d_cbias[:inner],
            d_ggain,
            d_dtbias,
            d_alog,
            d_skipped,
            d_wbc,
            d_cweight[:, inner:],
            d_cbias[inner:],
        )
    stacks = [
        jnp.stack([collected[layer_idx][member] for layer_idx in range(LAYERS)])
        for member in range(14)
    ]
    weight_sums = (
        lax.psum_scatter(
            stacks[0].astype(jnp.bfloat16), "seq", scatter_dimension=1, tiled=True
        ).astype(jnp.float32),
        lax.psum_scatter(
            stacks[1].astype(jnp.bfloat16), "seq", scatter_dimension=1, tiled=True
        ).astype(jnp.float32),
        lax.psum_scatter(
            stacks[2].astype(jnp.bfloat16), "seq", scatter_dimension=1, tiled=True
        ).astype(jnp.float32),
        lax.psum_scatter(
            stacks[3].astype(jnp.bfloat16), "seq", scatter_dimension=2, tiled=True
        ).astype(jnp.float32),
    )
    vector_sums = lax.psum(
        (stacks[4], stacks[5], stacks[6], stacks[7], stacks[8], stacks[9], stacks[10]), "seq"
    )
    shared_sums = lax.psum((stacks[11], stacks[12], stacks[13]), ("seq", "head"))
    return (
        hidden,
        grad,
        vector_sums[0],
        weight_sums[0],
        weight_sums[1],
        shared_sums[0],
        weight_sums[2],
        vector_sums[1],
        vector_sums[2],
        shared_sums[1],
        shared_sums[2],
        vector_sums[4],
        vector_sums[5],
        vector_sums[6],
        vector_sums[3],
        weight_sums[3],
    )


def solution(mesh):
    return jax.shard_map(
        local,
        mesh=mesh,
        in_specs=(
            P("seq", "head"),
            P(None, "head"),
            P(None, None, "head"),
            P(None, None, "head"),
            P(),
            P(None, None, "head"),
            P(None, None, "head"),
            P(None, "head"),
            P(),
            P(),
            P(None, "head"),
            P(None, "head"),
            P(None, "head"),
            P(None, "head"),
            P(None, "head", None),
            P("seq", "head"),
        ),
        out_specs=(
            P("seq", "head"),
            P("seq", "head"),
            P(None, "head"),
            P(None, "seq", "head"),
            P(None, "seq", "head"),
            P(),
            P(None, "seq", "head"),
            P(None, None, "head"),
            P(None, "head"),
            P(),
            P(),
            P(None, "head"),
            P(None, "head"),
            P(None, "head"),
            P(None, "head"),
            P(None, "head", "seq"),
        ),
        check_vma=False,
    )
```

profile of v0, /device:TPU:0, one launch (start us, length us, event | category | flops | bytes accessed | tf_op | source)
XLA Modules:
  0.0 995.1 jit_solution(10929443034664853142)
XLA Ops:
  22.1 6.9 all-gather.15.cloned.1.call-done
  45.5 21.2 %all-reduce.26 = f32[64]{0:T(128)S(1)} all-reduce(f32[64]{0:T(128)S(1)} %exponential_dynamic-update-slice_fusion.1), channel_id=3, replica_groups=mesh['seq'=8,'head'=4] {'seq'}, use_global_device_ids=true, to_apply=%add.26 | all-reduce | flops 64 | bytes 512
  68.5 23.3 %all-gather.19.cloned.1.call-done = f32[64,64,128]{2,1,0:T(8,128)} async-done(((f32[8,64,128]{2,1,0:T(8,128)}), f32[64,64,128]{2,1,0:T(8,128)}) %all-gather.19.cloned.1.call-update) | async-done | bytes 2097168 | tf_op jit(solution)/shard_map/all_gather | solution.py:25
  91.8 7.6 while.44
  117.8 23.7 %reduce-scatter.13.cloned.1.call-done = f32[256,256]{0,1:T(8,128)} async-done(((f32[1024,256]{0,1:T(8,128)}), f32[256,256]{0,1:T(8,128)}) %reduce-scatter.13.cloned.1.call-update) | async-done | bytes 262160 | tf_op jit(solution)/shard_map/reduce_scatter | solution.py:179
  149.6 10.6 %all-gather.17.cloned.1.call-done = f32[256,1024]{1,0:T(8,128)} async-done(((f32[256,256]{1,0:T(8,128)}), f32[256,1024]{1,0:T(8,128)}) %all-gather.17.cloned.1.call-update) | async-done | bytes 1048592 | tf_op jit(solution)/shard_map/all_gather | solution.py:141
  181.6 7.0 all_gather.64
  189.3 22.7 %all-reduce.27 = f32[64]{0:T(128)S(1)} all-reduce(f32[64]{0:T(128)S(1)} %exponential_dynamic-update-slice_fusion), channel_id=6, replica_groups=mesh['seq'=8,'head'=4] {'seq'}, use_global_device_ids=true, to_apply=%add.27 | all-reduce | flops 64 | bytes 512
  217.7 13.2 %all-gather.21.cloned.1.call-done = f32[64,64,128]{2,1,0:T(8,128)} async-done(((f32[8,64,128]{2,1,0:T(8,128)}), f32[64,64,128]{2,1,0:T(8,128)}) %all-gather.21.cloned.1.call-update) | async-done | bytes 2097168 | tf_op jit(solution)/shard_map/all_gather | solution.py:25
  230.9 15.9 %while.45 = (s32[]{:T(128)}, f32[8,64,128]{2,1,0:T(8,128)S(1)}, s32[]{:T(128)}, f32[8,8]{1,0:T(8,128)}, f32[8,8,64,128]{3,2,1,0:T(8,128)}, /*index=5*/s32[]{:T(128)}, s32[]{:T(128)}) while((s32[]{:T(128)}, f32[8,64,128]{2,1,0:T(8,128)S(1)}, s32[]{:T(128)}, f32[8,8]{1,0:T(8,128)}, f32[8,8,64,128]{3,2,1,0:T(8,128)}, ...), condition=%wide.region_14.16_spmd.clone, body=%wide.region_13.15_spmd.clone.sunk | while | flops 262148 | bytes 786633 | solution.py:37
  306.4 22.6 %all-gather.23.cloned.1.call-done = f32[64,64,128]{2,1,0:T(8,128)} async-done(((f32[8,64,128]{2,1,0:T(8,128)}), f32[64,64,128]{2,1,0:T(8,128)}) %all-gather.23.cloned.1.call-update) | async-done | bytes 2097168 | tf_op jit(solution)/shard_map/all_gather | solution.py:25
  332.1 15.8 %while.46 = (s32[]{:T(128)}, f32[8,64,128]{2,1,0:T(8,128)S(1)}, s32[]{:T(128)}, f32[8,8]{1,0:T(8,128)}, f32[8,8,64,128]{3,2,1,0:T(8,128)}, /*index=5*/s32[]{:T(128)}, s32[]{:T(128)}) while((s32[]{:T(128)}, f32[8,64,128]{2,1,0:T(8,128)S(1)}, s32[]{:T(128)}, f32[8,8]{1,0:T(8,128)}, f32[8,8,64,128]{3,2,1,0:T(8,128)}, ...), condition=%wide.region_22.24_spmd.clone, body=%wide.region_21.23_spmd.clone.sunk | while | flops 262148 | bytes 786633 | solution.py:37
  388.6 21.4 %reduce-scatter.17.cloned.1.call-done = f32[256,256]{0,1:T(8,128)} async-done(((f32[1024,256]{0,1:T(8,128)}), f32[256,256]{0,1:T(8,128)}) %reduce-scatter.17.cloned.1.call-update) | async-done | bytes 262160 | tf_op jit(solution)/shard_map/reduce_scatter | solution.py:278
  417.5 19.9 %reduce-scatter.15.cloned.1.call-done = f32[256,256]{0,1:T(8,128)} async-done(((f32[1024,256]{0,1:T(8,128)}), f32[256,256]{0,1:T(8,128)}) %reduce-scatter.15.cloned.1.call-update) | async-done | bytes 262160 | tf_op jit(solution)/shard_map/reduce_scatter | solution.py:179
  439.6 6.7 all_gather.67
  475.4 35.6 %all-gather.25.cloned.1.call-done = f32[64,64,128]{2,1,0:T(8,128)} async-done(((f32[8,64,128]{2,1,0:T(8,128)}), f32[64,64,128]{2,1,0:T(8,128)}) %all-gather.25.cloned.1.call-update) | async-done | bytes 2097168 | tf_op jit(solution)/shard_map/all_gather | solution.py:25
  514.2 12.3 %while.47 = (s32[]{:T(128)}, f32[8,64,128]{2,1,0:T(8,128)S(1)}, s32[]{:T(128)}, f32[8,8]{1,0:T(8,128)}, f32[8,8,64,128]{3,2,1,0:T(8,128)}, /*index=5*/s32[]{:T(128)}, s32[]{:T(128)}) while((s32[]{:T(128)}, f32[8,64,128]{2,1,0:T(8,128)S(1)}, s32[]{:T(128)}, f32[8,8]{1,0:T(8,128)}, f32[8,8,64,128]{3,2,1,0:T(8,128)}, ...), condition=%wide.region_43.45_spmd.clone, body=%wide.region_42.44_spmd.clone.sunk | while | flops 262148 | bytes 786633 | solution.py:37
  597.7 41.8 %all-reduce.28 = (f32[2,4,256]{2,1,0:T(4,128)}, f32[2,256]{1,0:T(2,128)}) all-reduce(f32[2,4,256]{2,1,0:T(4,128)S(1)} %pad_maximum_fusion.8, f32[2,256]{1,0:T(2,128)S(1)} %pad_maximum_fusion.16), channel_id=1, replica_groups=mesh['seq'=8,'head'=4] {'seq','head'}, use_global_device_ids=true, to_apply=%region_79.81 | all-reduce | flops 2560 | bytes 20480 | tf_op jit(solution)/shard_map/psum | solution.py:329
  643.6 31.7 %reduce-scatter.27.cloned.1.call-done = bf16[128,1024]{1,0:T(8,128)(2,1)} async-done(((bf16[1024,1024]{1,0:T(8,128)(2,1)}), bf16[128,1024]{1,0:T(8,128)(2,1)}) %reduce-scatter.27.cloned.1.call-update) | async-done | bytes 262160
  677.5 69.4 %reduce-scatter.21.cloned.1.call-done = bf16[2,128,512]{2,1,0:T(8,128)(2,1)} async-done(((bf16[2,1024,512]{2,1,0:T(8,128)(2,1)}), bf16[2,128,512]{2,1,0:T(8,128)(2,1)}) %reduce-scatter.21.cloned.1.call-update) | async-done | bytes 262160 | tf_op jit(solution)/shard_map/reduce_scatter | solution.py:313
  748.7 24.5 %reduce-scatter.19.cloned.1.call-done = f32[256,256]{0,1:T(8,128)} async-done(((f32[1024,256]{0,1:T(8,128)}), f32[256,256]{0,1:T(8,128)}) %reduce-scatter.19.cloned.1.call-update) | async-done | bytes 262160 | tf_op jit(solution)/shard_map/reduce_scatter | solution.py:278
  780.1 38.2 %all-reduce.29 = (f32[2,256]{1,0:T(2,128)}, f32[2,4,512]{2,1,0:T(4,128)}, f32[2,512]{1,0:T(2,128)}, f32[2,8]{1,0:T(2,128)}, f32[2,8]{1,0:T(2,128)}, /*index=5*/f32[2,8]{1,0:T(2,128)}, f32[2,512]{1,0:T(2,128)}) all-reduce(f32[2,256]{1,0:T(2,128)S(1)} %pad_maximum_fusion.15, ...), channel_id=1, replica_groups=mesh['seq'=8,'head'=4] {'seq'}, use_global_device_ids=true, to_apply=%region_62.64 | all-reduce | flops 6704 | bytes 53632 | tf_op jit(solution)/shard_map/psum | solution.py:326
  820.2 25.9 %reduce-scatter.23.cloned.1.call-done = bf16[2,128,512]{2,1,0:T(8,128)(2,1)} async-done(((bf16[2,1024,512]{2,1,0:T(8,128)(2,1)}), bf16[2,128,512]{2,1,0:T(8,128)(2,1)}) %reduce-scatter.23.cloned.1.call-update) | async-done | bytes 262160 | tf_op jit(solution)/shard_map/reduce_scatter | solution.py:316
  847.9 137.2 %all-reduce.32.cloned.1.call-done = f32[2,1024,256]{2,1,0:T(8,128)} async-done(((f32[2,1024,256]{2,1,0:T(8,128)}), f32[2,1024,256]{2,1,0:T(8,128)}) %all-reduce.32.cloned.1.call-update) | async-done | bytes 2097168 | tf_op jit(solution)/shard_map/psum | solution.py:329
  (638 shorter events, 374.0 us)
Async XLA Ops:
  7.2 21.8 %all-gather.15.cloned.1.call-start = ((), (), s32[]{:S(2)}) async-start(), calls=%async_computation.8 | async-start | bytes 1310720 | tf_op jit(solution)/shard_map/all_gather | solution.py:141
  7.9 83.9 %all-gather.19.cloned.1.call-start = ((), (), s32[]{:S(2)}) async-start(), calls=%async_computation.17 | async-start | bytes 2359296 | tf_op jit(solution)/shard_map/all_gather | solution.py:25
  8.7 134.5 %copy-start.103 = (f32[1,256]{1,0:T(1,128)}, f32[1,256]{1,0:T(1,128)S(1)}, u32[]{:S(2)}) copy-start(f32[1,256]{1,0:T(1,128)S(1)} %get-tuple-element.1312) | copy-start | bytes 3076
  32.9 6.0 collective-permute-start
  42.3 99.1 %reduce-scatter.13.cloned.1.call-start = ((), (), s32[]{:S(2)}) async-start(), calls=%async_computation.9 | async-start | bytes 1310720 | tf_op jit(solution)/shard_map/reduce_scatter | solution.py:179
  117.7 42.5 %all-gather.17.cloned.1.call-start = ((), (), s32[]{:S(2)}) async-start(), calls=%async_computation.10 | async-start | bytes 1310720 | tf_op jit(solution)/shard_map/all_gather | solution.py:141
  143.2 87.7 %all-gather.21.cloned.1.call-start = ((), (), s32[]{:S(2)}) async-start(), calls=%async_computation.18 | async-start | bytes 2359296 | tf_op jit(solution)/shard_map/all_gather | solution.py:25
  167.1 4.8 collective-permute-start.1
  180.5 148.4 %all-gather.23.cloned.1.call-start = ((), (), s32[]{:S(2)}) async-start(), calls=%async_computation.19 | async-start | bytes 2359296 | tf_op jit(solution)/shard_map/all_gather | solution.py:25
  281.6 128.5 %reduce-scatter.17.cloned.1.call-start = ((), (), s32[]{:S(2)}) async-start(), calls=%async_computation.12 | async-start | bytes 1310720 | tf_op jit(solution)/shard_map/reduce_scatter | solution.py:278
  376.8 5.6 collective-permute-start.2
  385.7 51.7 %reduce-scatter.15.cloned.1.call-start = ((), (), s32[]{:S(2)}) async-start(), calls=%async_computation.11 | async-start | bytes 1310720 | tf_op jit(solution)/shard_map/reduce_scatter | solution.py:179
  388.6 122.4 %all-gather.25.cloned.1.call-start = ((), (), s32[]{:S(2)}) async-start(), calls=%async_computation.20 | async-start | bytes 2359296 | tf_op jit(solution)/shard_map/all_gather | solution.py:25
  461.4 180.5 %reduce-scatter.25.cloned.1.call-start = ((), (), s32[]{:S(2)}) async-start(), calls=%async_computation.21 | async-start | bytes 294912
  543.1 132.2 %reduce-scatter.27.cloned.1.call-start = ((), (), s32[]{:S(2)}) async-start(), calls=%async_computation.22 | async-start | bytes 2359296
  555.9 191.0 %reduce-scatter.21.cloned.1.call-start = ((), (), s32[]{:S(2)}) async-start(), calls=%async_computation.14 | async-start | bytes 2359296 | tf_op jit(solution)/shard_map/reduce_scatter | solution.py:313
  560.2 213.0 %reduce-scatter.19.cloned.1.call-start = ((), (), s32[]{:S(2)}) async-start(), calls=%async_computation.13 | async-start | bytes 1310720 | tf_op jit(solution)/shard_map/reduce_scatter | solution.py:278
  583.2 5.9 collective-permute-start.3
  592.1 254.0 %reduce-scatter.23.cloned.1.call-start = ((), (), s32[]{:S(2)}) async-start(), calls=%async_computation.15 | async-start | bytes 2359296 | tf_op jit(solution)/shard_map/reduce_scatter | solution.py:316
  594.8 390.2 %all-reduce.32.cloned.1.call-start = ((), (), s32[]{:S(2)}) async-start(), calls=%async_computation.16 | async-start | bytes 4194304 | tf_op jit(solution)/shard_map/psum | solution.py:329
  641.9 131.4 %copy-start.102 = (f32[1,256]{1,0:T(1,128)S(1)}, f32[1,256]{1,0:T(1,128)}, u32[]{:S(2)}) copy-start(f32[1,256]{1,0:T(1,128)} %copy-done.101) | copy-start | bytes 3076
  641.9 131.4 %copy-start.109 = (f32[256]{0:T(256)S(1)}, f32[256]{0:T(256)}, u32[]{:S(2)}) copy-start(f32[256]{0:T(256)} %copy-done.108) | copy-start | bytes 3076
  641.9 138.2 %copy-start.123 = (f32[256]{0:T(256)S(1)}, f32[256]{0:T(256)}, u32[]{:S(2)}) copy-start(f32[256]{0:T(256)} %get-tuple-element.1182) | copy-start | bytes 3076
  641.9 176.5 %copy-start.55 = (f32[256,256]{1,0:T(8,128)S(1)}, f32[256,256]{1,0:T(8,128)}, u32[]{:S(2)}) copy-start(f32[256,256]{1,0:T(8,128)} %get-tuple-element.1264) | copy-start | bytes 786436
  (138 other events, 1824.1 us)
Sparse Core Ops, SparseCore 0:
  9.5 19.4 all-gather.14
  42.4 49.3 all-gather.18
  117.8 23.5 reduce-scatter.12
  143.4 16.6 all-gather.16
  180.7 50.1 all-gather.20
  281.7 47.2 all-gather.22
  385.8 24.1 reduce-scatter.16
  412.6 24.7 reduce-scatter.14
  461.5 49.4 all-gather.24
  543.2 60.5 reduce-scatter.24
  607.4 67.9 reduce-scatter.26
  679.3 67.6 reduce-scatter.20
  749.5 23.7 reduce-scatter.18
  776.6 69.4 reduce-scatter.22
  851.3 133.7 all-reduce.31
where the time goes:
time: 1010 us; the launch traced here: 995 us
  waiting for transfers between devices  475 us (47%)
  blocking collectives  185 us (18%)
  other arithmetic  110 us (11%)
  matrix products  100 us (10%)
  local copies, waits for them, and re-layouts  96.9 us (10%)
  between operations  17.1 us (2%)
  starting transfers between devices  10.5 us (1%)
    psum x1, waiting for transfers between devices, local(): lax.psum((stacks[11], stacks[12], stacks[13]), ('seq', 'head'))  137 us
    all_gather x4, waiting for transfers between devices, entering_2(): pieces = jax.tree.map(lambda part: lax.all_gather(part, axis), value)  94.6 us
    reduce_scatter x1, waiting for transfers between devices, local(): lax.psum_scatter(stacks[0].astype(jnp.bfloat16), 'seq', scatter_dimension...  69.4 us
    reduce_scatter x2, waiting for transfers between devices, local(): lax.psum_scatter(product(wz_now, d_gate_b) + product(wx_now, d_x_b) + pro...  45.9 us
    unnamed x2, blocking collectives  43.9 us
    reduce_scatter x2, waiting for transfers between devices, local(): lax.psum_scatter(contract_first(out_weight, scaled.T), 'head', scatter_di...  43.6 us
    psum x1, blocking collectives, local(): lax.psum((stacks[11], stacks[12], stacks[13]), ('seq', 'head'))  41.8 us
    psum x1, blocking collectives, local(): lax.psum((stacks[4], stacks[5], stacks[6], stacks[7], stacks[8], stacks[9...  38.2 us
  transfers between devices with their start and end apart: 19, of which 17 were waited for; matrix products, arithmetic and copies ran while one was open for 13% of the time, Pallas kernels for 0%

commit v1 on v0

--- a/solution.py
+++ b/solution.py
@@ -326,7 +326,9 @@
     vector_sums = lax.psum(
         (stacks[4], stacks[5], stacks[6], stacks[7], stacks[8], stacks[9], stacks[10]), "seq"
     )
-    shared_sums = lax.psum((stacks[11], stacks[12], stacks[13]), ("seq", "head"))
+    shared_sums = (stacks[11], stacks[12], stacks[13])
+    for hop_no in ("head", "seq"):
+        shared_sums = lax.psum(shared_sums, axis_name=hop_no)
     return (
         hidden,
         grad,

time: 1010 us -> 1050 us (1.040)
  waiting for transfers between devices: 475 us -> 550 us
  blocking collectives: 185 us -> 148 us
    unnamed x17 -> x18, waiting for transfers between devices: 32.7 us -> 136 us
    psum x1 -> x0, blocking collectives: 41.8 us -> none  [local(): lax.psum((stacks[11], stacks[12], stacks[13]), ('seq', 'head'))]
    psum x1 -> x2, waiting for transfers between devices: 137 us -> 124 us  [local(): shared_sums = lax.psum(shared_sums, axis_name=hop_no)]
    unnamed x300 -> x320, local copies, waits for them, and re-layouts: 26.8 us -> 25.3 us
  transfers between devices with their start and end apart: 19 -> 20, of which waited for: 17 -> 19; matrix products, arithmetic and copies ran while one was open for 13% -> 11% of each run, Pallas kernels for 0% -> 0%
where the time goes in v1:
time: 1050 us; the launch traced here: 1040 us
  waiting for transfers between devices  550 us (52%)
  blocking collectives  148 us (14%)
  other arithmetic  120 us (11%)
  matrix products  101 us (10%)
  local copies, waits for them, and re-layouts  95.4 us (9%)
  between operations  17.1 us (2%)
    unnamed x18, waiting for transfers between devices  136 us
    psum x2, waiting for transfers between devices, local(): shared_sums = lax.psum(shared_sums, axis_name=hop_no)  124 us
    all_gather x4, waiting for transfers between devices, entering_2(): pieces = jax.tree.map(lambda part: lax.all_gather(part, axis), value)  85.7 us
    reduce_scatter x1, waiting for transfers between devices, local(): lax.psum_scatter(stacks[0].astype(jnp.bfloat16), 'seq', scatter_dimension...  69.4 us
    reduce_scatter x2, waiting for transfers between devices, local(): lax.psum_scatter(product(wz_now, d_gate_b) + product(wx_now, d_x_b) + pro...  45.9 us
    unnamed x2, blocking collectives  43.7 us
    reduce_scatter x2, waiting for transfers between devices, local(): lax.psum_scatter(contract_first(out_weight, scaled.T), 'head', scatter_di...  43.6 us
    psum x6, blocking collectives, token_sums(): return lax.psum(partial_sums, 'head')  40.5 us
  transfers between devices with their start and end apart: 20, of which 19 were waited for; matrix products, arithmetic and copies ran while one was open for 11% of the time, Pallas kernels for 0%

profile of v1, /device:TPU:0, one launch (start us, length us, event | category | flops | bytes accessed | tf_op | source)
XLA Modules:
  0.0 1041.9 jit_solution(17778061843985212667)
XLA Ops:
  45.6 21.2 %all-reduce.26 = f32[64]{0:T(128)S(1)} all-reduce(f32[64]{0:T(128)S(1)} %exponential_dynamic-update-slice_fusion.1), channel_id=3, replica_groups=mesh['seq'=8,'head'=4] {'seq'}, use_global_device_ids=true, to_apply=%add.26 | all-reduce | flops 64 | bytes 512
  68.6 23.0 %all-gather.19.cloned.1.call-done = f32[64,64,128]{2,1,0:T(8,128)} async-done(((f32[8,64,128]{2,1,0:T(8,128)}), f32[64,64,128]{2,1,0:T(8,128)}) %all-gather.19.cloned.1.call-update) | async-done | bytes 2097168 | tf_op jit(solution)/shard_map/all_gather | solution.py:25
  91.6 7.6 while.44
  117.6 23.7 %reduce-scatter.13.cloned.1.call-done = f32[256,256]{0,1:T(8,128)} async-done(((f32[1024,256]{0,1:T(8,128)}), f32[256,256]{0,1:T(8,128)}) %reduce-scatter.13.cloned.1.call-update) | async-done | bytes 262160 | tf_op jit(solution)/shard_map/reduce_scatter | solution.py:179
  149.4 10.6 %all-gather.17.cloned.1.call-done = f32[256,1024]{1,0:T(8,128)} async-done(((f32[256,256]{1,0:T(8,128)}), f32[256,1024]{1,0:T(8,128)}) %all-gather.17.cloned.1.call-update) | async-done | bytes 1048592 | tf_op jit(solution)/shard_map/all_gather | solution.py:141
  189.1 22.5 %all-reduce.27 = f32[64]{0:T(128)S(1)} all-reduce(f32[64]{0:T(128)S(1)} %exponential_dynamic-update-slice_fusion), channel_id=6, replica_groups=mesh['seq'=8,'head'=4] {'seq'}, use_global_device_ids=true, to_apply=%add.27 | all-reduce | flops 64 | bytes 512
  217.4 13.3 %all-gather.21.cloned.1.call-done = f32[64,64,128]{2,1,0:T(8,128)} async-done(((f32[8,64,128]{2,1,0:T(8,128)}), f32[64,64,128]{2,1,0:T(8,128)}) %all-gather.21.cloned.1.call-update) | async-done | bytes 2097168 | tf_op jit(solution)/shard_map/all_gather | solution.py:25
  230.7 15.9 %while.45 = (s32[]{:T(128)}, f32[8,64,128]{2,1,0:T(8,128)S(1)}, s32[]{:T(128)}, f32[8,8]{1,0:T(8,128)}, f32[8,8,64,128]{3,2,1,0:T(8,128)}, /*index=5*/s32[]{:T(128)}, s32[]{:T(128)}) while((s32[]{:T(128)}, f32[8,64,128]{2,1,0:T(8,128)S(1)}, s32[]{:T(128)}, f32[8,8]{1,0:T(8,128)}, f32[8,8,64,128]{3,2,1,0:T(8,128)}, ...), condition=%wide.region_14.16_spmd.clone, body=%wide.region_13.15_spmd.clone.sunk | while | flops 262148 | bytes 786633 | solution.py:37
  306.2 22.5 %all-gather.23.cloned.1.call-done = f32[64,64,128]{2,1,0:T(8,128)} async-done(((f32[8,64,128]{2,1,0:T(8,128)}), f32[64,64,128]{2,1,0:T(8,128)}) %all-gather.23.cloned.1.call-update) | async-done | bytes 2097168 | tf_op jit(solution)/shard_map/all_gather | solution.py:25
  331.9 15.8 %while.46 = (s32[]{:T(128)}, f32[8,64,128]{2,1,0:T(8,128)S(1)}, s32[]{:T(128)}, f32[8,8]{1,0:T(8,128)}, f32[8,8,64,128]{3,2,1,0:T(8,128)}, /*index=5*/s32[]{:T(128)}, s32[]{:T(128)}) while((s32[]{:T(128)}, f32[8,64,128]{2,1,0:T(8,128)S(1)}, s32[]{:T(128)}, f32[8,8]{1,0:T(8,128)}, f32[8,8,64,128]{3,2,1,0:T(8,128)}, ...), condition=%wide.region_22.24_spmd.clone, body=%wide.region_21.23_spmd.clone.sunk | while | flops 262148 | bytes 786633 | solution.py:37
  358.7 13.6 %reduce-window.90 = f32[8,2,128]{2,0,1:T(8,128)S(1)} reduce-window(f32[8,2,128]{2,0,1:T(8,128)S(1)} %fusion.248, f32[]{:T(128)} %constant.312.clone.1), window={size=1x1x128 pad=0_0x0_0x0_127}, to_apply=%region_33.35 | reduce-window | flops 260096 | bytes 16388 | tf_op jit(solution)/shard_map/reduce-window.24
  399.3 21.4 %reduce-scatter.17.cloned.1.call-done = f32[256,256]{0,1:T(8,128)} async-done(((f32[1024,256]{0,1:T(8,128)}), f32[256,256]{0,1:T(8,128)}) %reduce-scatter.17.cloned.1.call-update) | async-done | bytes 262160 | tf_op jit(solution)/shard_map/reduce_scatter | solution.py:278
  428.1 19.9 %reduce-scatter.15.cloned.1.call-done = f32[256,256]{0,1:T(8,128)} async-done(((f32[1024,256]{0,1:T(8,128)}), f32[256,256]{0,1:T(8,128)}) %reduce-scatter.15.cloned.1.call-update) | async-done | bytes 262160 | tf_op jit(solution)/shard_map/reduce_scatter | solution.py:179
  494.8 26.9 %all-gather.25.cloned.1.call-done = f32[64,64,128]{2,1,0:T(8,128)} async-done(((f32[8,64,128]{2,1,0:T(8,128)}), f32[64,64,128]{2,1,0:T(8,128)}) %all-gather.25.cloned.1.call-update) | async-done | bytes 2097168 | tf_op jit(solution)/shard_map/all_gather | solution.py:25
  524.8 12.5 %while.47 = (s32[]{:T(128)}, f32[8,64,128]{2,1,0:T(8,128)S(1)}, s32[]{:T(128)}, f32[8,8]{1,0:T(8,128)}, f32[8,8,64,128]{3,2,1,0:T(8,128)}, /*index=5*/s32[]{:T(128)}, s32[]{:T(128)}) while((s32[]{:T(128)}, f32[8,64,128]{2,1,0:T(8,128)S(1)}, s32[]{:T(128)}, f32[8,8]{1,0:T(8,128)}, f32[8,8,64,128]{3,2,1,0:T(8,128)}, ...), condition=%wide.region_43.45_spmd.clone, body=%wide.region_42.44_spmd.clone.sunk | while | flops 262148 | bytes 786633 | solution.py:37
  598.9 20.8 %all-reduce.33.cloned.1.call-done = f32[2,1024,256]{2,1,0:T(8,128)} async-done(((f32[2,1024,256]{2,1,0:T(8,128)}), f32[2,1024,256]{2,1,0:T(8,128)}) %all-reduce.33.cloned.1.call-update) | async-done | bytes 2097168 | tf_op jit(solution)/shard_map/psum | solution.py:331
  620.4 65.5 %reduce-scatter.25.cloned.1.call-done = bf16[128,16]{1,0:T(8,128)(2,1)} async-done(((bf16[1024,16]{1,0:T(8,128)(2,1)}), bf16[128,16]{1,0:T(8,128)(2,1)}) %reduce-scatter.25.cloned.1.call-update) | async-done | bytes 4112
  687.4 69.3 %reduce-scatter.27.cloned.1.call-done = bf16[128,1024]{1,0:T(8,128)(2,1)} async-done(((bf16[1024,1024]{1,0:T(8,128)(2,1)}), bf16[128,1024]{1,0:T(8,128)(2,1)}) %reduce-scatter.27.cloned.1.call-update) | async-done | bytes 262160
  758.9 69.4 %reduce-scatter.21.cloned.1.call-done = bf16[2,128,512]{2,1,0:T(8,128)(2,1)} async-done(((bf16[2,1024,512]{2,1,0:T(8,128)(2,1)}), bf16[2,128,512]{2,1,0:T(8,128)(2,1)}) %reduce-scatter.21.cloned.1.call-update) | async-done | bytes 262160 | tf_op jit(solution)/shard_map/reduce_scatter | solution.py:313
  830.1 24.5 %reduce-scatter.19.cloned.1.call-done = f32[256,256]{0,1:T(8,128)} async-done(((f32[1024,256]{0,1:T(8,128)}), f32[256,256]{0,1:T(8,128)}) %reduce-scatter.19.cloned.1.call-update) | async-done | bytes 262160 | tf_op jit(solution)/shard_map/reduce_scatter | solution.py:278
  855.7 10.1 all-reduce.29
  865.8 38.5 %all-reduce.28 = (f32[2,256]{1,0:T(2,128)}, f32[2,4,512]{2,1,0:T(4,128)}, f32[2,512]{1,0:T(2,128)}, f32[2,4,256]{2,1,0:T(4,128)}, f32[2,256]{1,0:T(2,128)}, /*in...) all-reduce(f32[2,256]{1,0:T(2,128)S(1)} %pad_maximum_fusion.15, ...), channel_id=1, replica_groups=mesh['seq'=8,'head'=4] {'seq'}, use_global_device_ids=true, to_apply=%region_62.64 | all-reduce | flops 9264 | bytes 74112 | tf_op jit(solution)/shard_map/psum | solution.py:326
  906.1 20.9 %reduce-scatter.23.cloned.1.call-done = bf16[2,128,512]{2,1,0:T(8,128)(2,1)} async-done(((bf16[2,1024,512]{2,1,0:T(8,128)(2,1)}), bf16[2,128,512]{2,1,0:T(8,128)(2,1)}) %reduce-scatter.23.cloned.1.call-update) | async-done | bytes 262160 | tf_op jit(solution)/shard_map/reduce_scatter | solution.py:316
  928.9 103.0 %all-reduce.35.cloned.1.call-done = f32[2,1024,256]{2,1,0:T(8,128)} async-done(((f32[2,1024,256]{2,1,0:T(8,128)}), f32[2,1024,256]{2,1,0:T(8,128)}) %all-reduce.35.cloned.1.call-update) | async-done | bytes 2097168 | tf_op jit(solution)/shard_map/psum | solution.py:331
  (660 shorter events, 383.4 us)
Async XLA Ops:
  7.2 21.8 %all-gather.15.cloned.1.call-start = ((), (), s32[]{:S(2)}) async-start(), calls=%async_computation.8 | async-start | bytes 1310720 | tf_op jit(solution)/shard_map/all_gather | solution.py:141
  7.9 83.7 %all-gather.19.cloned.1.call-start = ((), (), s32[]{:S(2)}) async-start(), calls=%async_computation.18 | async-start | bytes 2359296 | tf_op jit(solution)/shard_map/all_gather | solution.py:25
  32.9 6.1 collective-permute-start
  42.4 98.9 %reduce-scatter.13.cloned.1.call-start = ((), (), s32[]{:S(2)}) async-start(), calls=%async_computation.9 | async-start | bytes 1310720 | tf_op jit(solution)/shard_map/reduce_scatter | solution.py:179
  117.5 42.5 %all-gather.17.cloned.1.call-start = ((), (), s32[]{:S(2)}) async-start(), calls=%async_computation.10 | async-start | bytes 1310720 | tf_op jit(solution)/shard_map/all_gather | solution.py:141
  143.0 87.7 %all-gather.21.cloned.1.call-start = ((), (), s32[]{:S(2)}) async-start(), calls=%async_computation.19 | async-start | bytes 2359296 | tf_op jit(solution)/shard_map/all_gather | solution.py:25
  166.9 4.8 collective-permute-start.1
  180.4 148.3 %all-gather.23.cloned.1.call-start = ((), (), s32[]{:S(2)}) async-start(), calls=%async_computation.20 | async-start | bytes 2359296 | tf_op jit(solution)/shard_map/all_gather | solution.py:25
  281.4 139.3 %reduce-scatter.17.cloned.1.call-start = ((), (), s32[]{:S(2)}) async-start(), calls=%async_computation.12 | async-start | bytes 1310720 | tf_op jit(solution)/shard_map/reduce_scatter | solution.py:278
  387.5 5.6 collective-permute-start.2
  396.4 51.7 %reduce-scatter.15.cloned.1.call-start = ((), (), s32[]{:S(2)}) async-start(), calls=%async_computation.11 | async-start | bytes 1310720 | tf_op jit(solution)/shard_map/reduce_scatter | solution.py:179
  399.2 122.4 %all-gather.25.cloned.1.call-start = ((), (), s32[]{:S(2)}) async-start(), calls=%async_computation.21 | async-start | bytes 2359296 | tf_op jit(solution)/shard_map/all_gather | solution.py:25
  472.1 147.7 %all-reduce.33.cloned.1.call-start = ((), (), s32[]{:S(2)}) async-start(), calls=%async_computation.16 | async-start | bytes 4194304 | tf_op jit(solution)/shard_map/psum | solution.py:331
  558.5 5.6 collective-permute-start.3
  568.8 117.1 %reduce-scatter.25.cloned.1.call-start = ((), (), s32[]{:S(2)}) async-start(), calls=%async_computation.22 | async-start | bytes 294912
  573.9 182.8 %reduce-scatter.27.cloned.1.call-start = ((), (), s32[]{:S(2)}) async-start(), calls=%async_computation.23 | async-start | bytes 2359296
  586.8 241.5 %reduce-scatter.21.cloned.1.call-start = ((), (), s32[]{:S(2)}) async-start(), calls=%async_computation.14 | async-start | bytes 2359296 | tf_op jit(solution)/shard_map/reduce_scatter | solution.py:313
  590.2 264.4 %reduce-scatter.19.cloned.1.call-start = ((), (), s32[]{:S(2)}) async-start(), calls=%async_computation.13 | async-start | bytes 1310720 | tf_op jit(solution)/shard_map/reduce_scatter | solution.py:278
  595.4 331.6 %reduce-scatter.23.cloned.1.call-start = ((), (), s32[]{:S(2)}) async-start(), calls=%async_computation.15 | async-start | bytes 2359296 | tf_op jit(solution)/shard_map/reduce_scatter | solution.py:316
  598.1 433.8 %all-reduce.35.cloned.1.call-start = ((), (), s32[]{:S(2)}) async-start(), calls=%async_computation.17 | async-start | bytes 4194304 | tf_op jit(solution)/shard_map/psum | solution.py:331
  619.8 234.8 %copy-start.104 = (f32[1,256]{1,0:T(1,128)S(1)}, f32[1,256]{1,0:T(1,128)}, u32[]{:S(2)}) copy-start(f32[1,256]{1,0:T(1,128)} %copy-done.103) | copy-start | bytes 3076
  619.8 234.8 %copy-start.111 = (f32[256]{0:T(256)S(1)}, f32[256]{0:T(256)}, u32[]{:S(2)}) copy-start(f32[256]{0:T(256)} %copy-done.110) | copy-start | bytes 3076
  619.8 246.0 %copy-start.131 = (f32[256]{0:T(256)S(1)}, f32[256]{0:T(256)}, u32[]{:S(2)}) copy-start(f32[256]{0:T(256)} %get-tuple-element.1182) | copy-start | bytes 3076
  619.8 284.5 %copy-start.56 = (f32[256,256]{1,0:T(8,128)S(1)}, f32[256,256]{1,0:T(8,128)}, u32[]{:S(2)}) copy-start(f32[256,256]{1,0:T(8,128)} %get-tuple-element.1267) | copy-start | bytes 786436
  (149 other events, 1907.5 us)
Sparse Core Ops, SparseCore 0:
  9.5 19.4 all-gather.14
  42.5 49.0 all-gather.18
  117.6 23.5 reduce-scatter.12
  143.3 16.6 all-gather.16
  180.5 50.1 all-gather.20
  281.6 47.0 all-gather.22
  396.5 24.1 reduce-scatter.16
  423.2 24.7 reduce-scatter.14
  472.2 49.4 all-gather.24
  568.9 50.8 all-reduce.32
  623.7 62.1 reduce-scatter.24
  689.2 67.4 reduce-scatter.26
  760.8 67.4 reduce-scatter.20
  830.7 23.8 reduce-scatter.18
  857.9 69.0 reduce-scatter.22
  930.5 101.2 all-reduce.34
